TPU v7x, 32 devices: a whole 2x2x4 slice. The times are simulated.
32 devices in a mesh: dp: 8 (over y, x, core), tensor: 4 (over z).
Axes of the slice: x: 2, y: 2, z: 4, core: 2. Of those that a mesh axis runs over, the one named last changes fastest.
Arguments:
- tokens: bfloat16 [16, 577, 1024], P('dp', None, 'tensor'), may hold values from -6 to 6
- cotangent: float32 [16, 577, 1024], P('dp', None, 'tensor'), may hold values from -6 to 6
- image_counts: int32 [8], P('dp'), may hold values from 1 to 2, as said below
- w_qkv: float32 [2, 1024, 3, 1024], P(None, 'dp', None, 'tensor'), as said below
- w_out: float32 [2, 1024, 1024], P(None, 'dp', 'tensor'), may hold values from -0.75 to 0.75
- w_fc1: float32 [2, 1024, 4096], P(None, 'dp', 'tensor'), may hold values from -0.1875 to 0.1875
- w_fc2: float32 [2, 1024, 4096], P(None, 'dp', 'tensor'), may hold values from -0.09375 to 0.09375
- vec_small: float32 [2, 8, 1024], P(None, None, 'tensor'), as said below
- fc1_bias: float32 [2, 4096], P(None, 'tensor'), may hold values from -3 to 3
- mom_qkv: float32 [2, 2, 1024, 3, 1024], P(None, None, 'dp', None, 'tensor'), as said below
- mom_out: float32 [2, 2, 1024, 1024], P(None, None, 'dp', 'tensor'), as said below
- mom_fc1: float32 [2, 2, 1024, 4096], P(None, None, 'dp', 'tensor'), as said below
- mom_fc2: float32 [2, 2, 1024, 4096], P(None, None, 'dp', 'tensor'), as said below
- mom_vec: float32 [2, 2, 8, 1024], P(None, None, None, 'tensor'), as said below
- mom_bias: float32 [2, 2, 4096], P(None, None, 'tensor'), as said below
Outputs:
- output: float32 [16, 577, 1024], P('dp', None, 'tensor')
- input_grad: float32 [16, 577, 1024], P('dp', None, 'tensor')
- grad_qkv: float32 [2, 1024, 3, 1024], P(None, 'dp', None, 'tensor')
- grad_out: float32 [2, 1024, 1024], P(None, 'dp', 'tensor')
- grad_fc1: float32 [2, 1024, 4096], P(None, 'dp', 'tensor')
- grad_fc2: float32 [2, 1024, 4096], P(None, 'dp', 'tensor')
- grad_vec: float32 [2, 8, 1024], P(None, None, 'tensor')
- grad_bias: float32 [2, 4096], P(None, 'tensor')
- new_qkv: float32 [2, 1024, 3, 1024], P(None, 'dp', None, 'tensor')
- new_out: float32 [2, 1024, 1024], P(None, 'dp', 'tensor')
- new_fc1: float32 [2, 1024, 4096], P(None, 'dp', 'tensor')
- new_fc2: float32 [2, 1024, 4096], P(None, 'dp', 'tensor')
- new_vec: float32 [2, 8, 1024], P(None, None, 'tensor')
- new_bias: float32 [2, 4096], P(None, 'tensor')
- newmom_qkv: float32 [2, 2, 1024, 3, 1024], P(None, None, 'dp', None, 'tensor')
- newmom_out: float32 [2, 2, 1024, 1024], P(None, None, 'dp', 'tensor')
- newmom_fc1: float32 [2, 2, 1024, 4096], P(None, None, 'dp', 'tensor')
- newmom_fc2: float32 [2, 2, 1024, 4096], P(None, None, 'dp', 'tensor')
- newmom_vec: float32 [2, 2, 8, 1024], P(None, None, None, 'tensor')
- newmom_bias: float32 [2, 2, 4096], P(None, None, 'tensor')
Inputs may be any that keep to these rules, and one draw needn't show every extreme that they name: Every index of dp holds 1 or 2 images; some index holds 2 and some holds 1. Slot 2 i always holds an image, slot 2 i + 1 only where image_counts[i] is 2; other slots' tokens and cotangents are ignored. `w_qkv`: independent entries of mean 0 and deviation 1024^-0.5. `vec_small`: gains and shifts of order one. `mom_qkv`: second moments (index 1 of dimension 0) are positive. `mom_out`: second moments (index 1 of dimension 0) are positive. `mom_fc1`: second moments (index 1 of dimension 0) are positive. `mom_fc2`: second moments (index 1 of dimension 0) are positive. `mom_vec`: second moments (index 1 of dimension 0) are positive. `mom_bias`: second moments (index 1 of dimension 0) are positive.
All inputs are finite; a program needn't handle non-finite values.
Results may differ from a plain program's by a relative error of at most 0.022.
Values may be sent and summed in bfloat16 or wider, within the bound.
A program may use at most 256 MiB of HBM per device.

v0:
```python
import jax
import jax.numpy as jnp
from jax import lax
from jax.sharding import PartitionSpec as P

D = 1024
HEADS = 16
LAYERS = 2
STEP = 10
NORM_EPS = 1e-06
ROOT_HALF = 0.7071067811865476
INV_ROOT_TWO_PI = 0.3989422804014327
LEARN_RATE = 0.01
BETA_ONE = 0.9
BETA_TWO = 0.999
ADAM_EPS = 1e-08
WEIGHT_DECAY = 0.05
CONTRACT_LAST = (((1,), (1,)), ((), ()))
CONTRACT_FIRST = (((0,), (0,)), ((), ()))


def as_sent(shard):
    return jax.tree.map(lambda a: a.astype(jnp.bfloat16) if a.dtype == jnp.float32 else a, shard)


def gelu_value(preactivation):
    return 0.5 * preactivation * (1.0 + jax.scipy.special.erf(preactivation * ROOT_HALF))


def gelu_slope(preactivation):
    return (
        0.5 * (1.0 + jax.scipy.special.erf(preactivation * ROOT_HALF))
        + preactivation * jnp.exp(-0.5 * preactivation * preactivation) * INV_ROOT_TWO_PI
    )


def layer_statistics(hidden_state):
    totals = lax.psum(
        (jnp.sum(hidden_state, -1), jnp.sum(hidden_state * hidden_state, -1)), "tensor"
    )
    mean_row = totals[0][..., None] / D
    spread = totals[1][..., None] / D - mean_row * mean_row
    inv_std = lax.rsqrt(spread + NORM_EPS)
    return ((hidden_state - mean_row) * inv_std, inv_std)


def norm_back(d_normed, normed, inv_std, gain, carried):
    d_hat = d_normed * gain
    totals = lax.psum((jnp.sum(d_hat, -1), jnp.sum(d_hat * normed, -1)), "tensor")
    grad_in = carried + inv_std * (
        d_hat - totals[0][..., None] / D - normed * totals[1][..., None] / D
    )
    return (grad_in, jnp.sum(d_normed * normed, (0, 1)), jnp.sum(d_normed, (0, 1)))


def share_features(local_rows):
    return lax.all_gather(local_rows, "tensor", axis=2, tiled=True)


def sum_branch(partial_rows):
    return lax.psum_scatter(partial_rows, "tensor", scatter_dimension=2, tiled=True)


def share_grads(local_rows):
    return lax.all_gather(local_rows, "tensor", axis=2, tiled=True)


def sum_inputs(partial_rows):
    return lax.psum_scatter(
        partial_rows.astype(jnp.bfloat16), "tensor", scatter_dimension=2, tiled=True
    ).astype(jnp.float32)


def fetch_weights(w_qkv, w_out, w_fc1, w_fc2, layer_number):
    pieces = (
        w_qkv[layer_number].astype(jnp.bfloat16),
        w_out[layer_number].astype(jnp.bfloat16),
        w_fc1[layer_number].astype(jnp.bfloat16),
        w_fc2[layer_number].astype(jnp.bfloat16),
    )
    return (
        lax.all_gather(pieces[0], "dp", axis=0, tiled=True),
        lax.all_gather(pieces[1], "dp", axis=0, tiled=True),
        lax.all_gather(pieces[2], "dp", axis=0, tiled=True),
        lax.all_gather(pieces[3], "dp", axis=0, tiled=True),
    )


def attend_forward(query_h, key_h, value_h, attn_scale):
    scores = (
        jnp.einsum("bqhd,bkhd->bhqk", query_h, key_h, preferred_element_type=jnp.float32)
        * attn_scale
    )
    top_score = jnp.max(scores, -1, keepdims=True)
    logged_total = top_score + jnp.log(jnp.sum(jnp.exp(scores - top_score), -1, keepdims=True))
    probs = jnp.exp(scores - logged_total).astype(jnp.bfloat16)
    attention_result = jnp.einsum(
        "bhqk,bkhd->bqhd", probs, value_h, preferred_element_type=jnp.float32
    ).astype(jnp.bfloat16)
    return (attention_result, logged_total)


def attend_backward(query_h, key_h, value_h, attention_result, d_att, logged_total, attn_scale):
    scores = (
        jnp.einsum("bqhd,bkhd->bhqk", query_h, key_h, preferred_element_type=jnp.float32)
        * attn_scale
    )
    probs = jnp.exp(scores - logged_total)
    probs_low = probs.astype(jnp.bfloat16)
    d_value = jnp.einsum("bhqk,bqhd->bkhd", probs_low, d_att, preferred_element_type=jnp.float32)
    d_probs = jnp.einsum("bqhd,bkhd->bhqk", d_att, value_h, preferred_element_type=jnp.float32)
    delta = jnp.sum(d_att.astype(jnp.float32) * attention_result.astype(jnp.float32), -1)
    d_scores = (probs * (d_probs - jnp.swapaxes(delta, 1, 2)[..., None]) * attn_scale).astype(
        jnp.bfloat16
    )
    d_query = jnp.einsum("bhqk,bkhd->bqhd", d_scores, key_h, preferred_element_type=jnp.float32)
    d_key = jnp.einsum("bhqk,bqhd->bkhd", d_scores, query_h, preferred_element_type=jnp.float32)
    return (d_query, d_key, d_value)


def adam_update(param, running_gradient, moments, decay):
    first = BETA_ONE * moments[0] + (1.0 - BETA_ONE) * running_gradient
    second = BETA_TWO * moments[1] + (1.0 - BETA_TWO) * running_gradient * running_gradient
    fix_one = 1.0 - BETA_ONE**STEP
    fix_two = 1.0 - BETA_TWO**STEP
    update = first / fix_one / (jnp.sqrt(second / fix_two) + ADAM_EPS) + decay * param
    return (param - LEARN_RATE * update, jnp.stack([first, second]))


def on_device(
    tokens,
    cotangent,
    image_counts,
    w_qkv,
    w_out,
    w_fc1,
    w_fc2,
    vec_small,
    fc1_bias,
    mom_qkv,
    mom_out,
    mom_fc1,
    mom_fc2,
    mom_vec,
    mom_bias,
):
    slot_count, seq_len, feat_width = tokens.shape
    tok_rows = slot_count * seq_len
    heads_here = HEADS // lax.axis_size("tensor")
    head_dim = feat_width // heads_here
    attn_scale = head_dim ** (-0.5)
    slot_live = jnp.stack([jnp.ones((), jnp.float32), (image_counts[0] == 2).astype(jnp.float32)])[
        :, None, None
    ]

    def to_heads(matrix):
        return matrix.reshape(slot_count, seq_len, heads_here, head_dim)

    def to_slots(matrix):
        return matrix.reshape(slot_count, seq_len, -1)

    hidden_state = tokens.astype(jnp.float32)
    saved_tensors = []
    fetched = []
    for layer_number in range(LAYERS):
        weights = fetch_weights(w_qkv, w_out, w_fc1, w_fc2, layer_number)
        fetched.append(weights)
        projection_weight, backward_weight, first_weight, second_weight = weights
        vector_rows = vec_small[layer_number]
        first_centered_scaled, first_inverse_deviation = layer_statistics(hidden_state)
        first_normalized = share_features(
            (first_centered_scaled * vector_rows[0] + vector_rows[1]).astype(jnp.bfloat16)
        ).reshape(tok_rows, -1)
        proj_out = lax.dot_general(
            first_normalized,
            projection_weight,
            (((1,), (0,)), ((), ())),
            preferred_element_type=jnp.float32,
        )
        query_matrix_rows = (proj_out[:, 0] + vector_rows[2]).astype(jnp.bfloat16)
        key_matrix_rows = proj_out[:, 1].astype(jnp.bfloat16)
        value_matrix_rows = (proj_out[:, 2] + vector_rows[3]).astype(jnp.bfloat16)
        attention_result, logged_total = attend_forward(
            to_heads(query_matrix_rows),
            to_heads(key_matrix_rows),
            to_heads(value_matrix_rows),
            attn_scale,
        )
        attention_result = attention_result.reshape(tok_rows, feat_width)
        attn_branch = sum_branch(
            to_slots(
                lax.dot_general(
                    attention_result,
                    backward_weight,
                    CONTRACT_LAST,
                    preferred_element_type=jnp.float32,
                )
            )
        )
        middle_state = hidden_state + attn_branch + vector_rows[4]
        second_centered_scaled, second_inverse_deviation = layer_statistics(middle_state)
        second_normalized = share_features(
            (second_centered_scaled * vector_rows[5] + vector_rows[6]).astype(jnp.bfloat16)
        ).reshape(tok_rows, -1)
        preactivation = (
            jnp.dot(second_normalized, first_weight, preferred_element_type=jnp.float32)
            + fc1_bias[layer_number]
        )
        activation_narrow = gelu_value(preactivation).astype(jnp.bfloat16)
        branch_two = lax.dot_general(
            activation_narrow, second_weight, CONTRACT_LAST, preferred_element_type=jnp.float32
        )
        new_hidden = middle_state + sum_branch(to_slots(branch_two)) + vector_rows[7]
        saved_tensors.append(
            (
                first_centered_scaled,
                first_inverse_deviation,
                first_normalized,
                query_matrix_rows,
                key_matrix_rows,
                value_matrix_rows,
                attention_result,
                logged_total,
                second_centered_scaled,
                second_inverse_deviation,
                second_normalized,
                preactivation,
                activation_narrow,
            )
        )
        hidden_state = new_hidden
    output = hidden_state * slot_live
    running_gradient = cotangent * slot_live
    big_grads = [None] * LAYERS
    vec_grads = [None] * LAYERS
    bias_grads = [None] * LAYERS
    for layer_number in reversed(range(LAYERS)):
        projection_weight, backward_weight, first_weight, second_weight = fetch_weights(
            w_qkv, w_out, w_fc1, w_fc2, layer_number
        )
        vector_rows = vec_small[layer_number]
        (
            first_centered_scaled,
            first_inverse_deviation,
            first_normalized,
            query_matrix_rows,
            key_matrix_rows,
            value_matrix_rows,
            attention_result,
            logged_total,
            second_centered_scaled,
            second_inverse_deviation,
            second_normalized,
            preactivation,
            activation_narrow,
        ) = saved_tensors[layer_number]
        full_grad = share_grads(running_gradient.astype(jnp.bfloat16)).reshape(tok_rows, -1)
        g_fc2 = lax.dot_general(
            full_grad, activation_narrow, CONTRACT_FIRST, preferred_element_type=jnp.float32
        )
        g_bias_two = jnp.sum(running_gradient, (0, 1))
        d_pre = jnp.dot(full_grad, second_weight, preferred_element_type=jnp.float32) * gelu_slope(
            preactivation
        )
        d_pre_low = d_pre.astype(jnp.bfloat16)
        g_fc1 = lax.dot_general(
            second_normalized, d_pre_low, CONTRACT_FIRST, preferred_element_type=jnp.float32
        )
        g_fc1_bias = jnp.sum(d_pre, 0)
        second_normed_gradient = sum_inputs(
            to_slots(
                lax.dot_general(
                    d_pre_low, first_weight, CONTRACT_LAST, preferred_element_type=jnp.float32
                )
            )
        )
        middle_gradient, second_gain_gradient, second_shift_gradient = norm_back(
            second_normed_gradient,
            second_centered_scaled,
            second_inverse_deviation,
            vector_rows[5],
            running_gradient,
        )
        full_mid = share_grads(middle_gradient.astype(jnp.bfloat16)).reshape(tok_rows, -1)
        g_out = lax.dot_general(
            full_mid, attention_result, CONTRACT_FIRST, preferred_element_type=jnp.float32
        )
        g_bias_out = jnp.sum(middle_gradient, (0, 1))
        d_att = jnp.dot(full_mid, backward_weight, preferred_element_type=jnp.float32).astype(
            jnp.bfloat16
        )
        d_query, d_key, d_value = attend_backward(
            to_heads(query_matrix_rows),
            to_heads(key_matrix_rows),
            to_heads(value_matrix_rows),
            to_heads(attention_result),
            to_heads(d_att),
            logged_total,
            attn_scale,
        )
        d_query = d_query.reshape(tok_rows, feat_width)
        d_key = d_key.reshape(tok_rows, feat_width)
        d_value = d_value.reshape(tok_rows, feat_width)
        d_proj = jnp.stack([d_query, d_key, d_value], axis=1).astype(jnp.bfloat16)
        g_qkv = lax.dot_general(
            first_normalized, d_proj, CONTRACT_FIRST, preferred_element_type=jnp.float32
        )
        first_normed_gradient = sum_inputs(
            to_slots(
                lax.dot_general(
                    d_proj,
                    projection_weight,
                    (((1, 2), (1, 2)), ((), ())),
                    preferred_element_type=jnp.float32,
                )
            )
        )
        running_gradient, first_gain_gradient, first_shift_gradient = norm_back(
            first_normed_gradient,
            first_centered_scaled,
            first_inverse_deviation,
            vector_rows[0],
            middle_gradient,
        )
        vec_grads[layer_number] = jnp.stack(
            [
                first_gain_gradient,
                first_shift_gradient,
                jnp.sum(d_query, 0),
                jnp.sum(d_value, 0),
                g_bias_out,
                second_gain_gradient,
                second_shift_gradient,
                g_bias_two,
            ]
        )
        bias_grads[layer_number] = g_fc1_bias
        layer_tuple = (g_qkv, g_out, g_fc1, g_fc2)
        big_grads[layer_number] = layer_tuple
    input_grad = running_gradient * slot_live
    stacked = tuple((jnp.stack([entry[which] for entry in big_grads]) for which in range(4)))
    stacked = jax.tree.map(
        lambda part: part.astype(jnp.float32),
        lax.psum_scatter(as_sent(stacked), "dp", scatter_dimension=1, tiled=True),
    )
    small_sums = lax.psum((jnp.stack(vec_grads), jnp.stack(bias_grads)), "dp")
    grad_totals = (stacked[0], stacked[1], stacked[2], stacked[3], small_sums[0], small_sums[1])
    params = (w_qkv, w_out, w_fc1, w_fc2, vec_small, fc1_bias)
    moments = (mom_qkv, mom_out, mom_fc1, mom_fc2, mom_vec, mom_bias)
    decays = (WEIGHT_DECAY, WEIGHT_DECAY, WEIGHT_DECAY, WEIGHT_DECAY, 0.0, 0.0)
    results = [
        adam_update(param, grad_total, moment, decay)
        for param, grad_total, moment, decay in zip(params, grad_totals, moments, decays)
    ]
    return (
        output,
        input_grad,
        grad_totals[0],
        grad_totals[1],
        grad_totals[2],
        grad_totals[3],
        grad_totals[4],
        grad_totals[5],
        results[0][0],
        results[1][0],
        results[2][0],
        results[3][0],
        results[4][0],
        results[5][0],
        results[0][1],
        results[1][1],
        results[2][1],
        results[3][1],
        results[4][1],
        results[5][1],
    )


def solution(mesh):
    return jax.shard_map(
        on_device,
        mesh=mesh,
        in_specs=(
            P("dp", None, "tensor"),
            P("dp", None, "tensor"),
            P("dp"),
            P(None, "dp", None, "tensor"),
            P(None, "dp", "tensor"),
            P(None, "dp", "tensor"),
            P(None, "dp", "tensor"),
            P(None, None, "tensor"),
            P(None, "tensor"),
            P(None, None, "dp", None, "tensor"),
            P(None, None, "dp", "tensor"),
            P(None, None, "dp", "tensor"),
            P(None, None, "dp", "tensor"),
            P(None, None, None, "tensor"),
            P(None, None, "tensor"),
        ),
        out_specs=(
            P("dp", None, "tensor"),
            P("dp", None, "tensor"),
            P(None, "dp", None, "tensor"),
            P(None, "dp", "tensor"),
            P(None, "dp", "tensor"),
            P(None, "dp", "tensor"),
            P(None, None, "tensor"),
            P(None, "tensor"),
            P(None, "dp", None, "tensor"),
            P(None, "dp", "tensor"),
            P(None, "dp", "tensor"),
            P(None, "dp", "tensor"),
            P(None, None, "tensor"),
            P(None, "tensor"),
            P(None, None, "dp", None, "tensor"),
            P(None, None, "dp", "tensor"),
            P(None, None, "dp", "tensor"),
            P(None, None, "dp", "tensor"),
            P(None, None, None, "tensor"),
            P(None, None, "tensor"),
        ),
        check_vma=False,
    )
```

profile of v0, /device:TPU:0, one launch (start us, length us, event | category | flops | bytes accessed | tf_op | source)
XLA Modules:
  0.0 1669.3 jit_solution(3100951194035109462)
XLA Ops:
  9.8 20.6 %all-reduce.8 = (f32[2,577]{1,0:T(2,128)S(1)}, f32[2,577]{1,0:T(2,128)S(1)}) all-reduce(f32[2,577]{1,0:T(2,128)S(1)} %get-tuple-element.103, f32[2,577]{1,0:T(2,128)S(1)} %get-tuple-element.102), channel_id=1, replica_groups=mesh['dp'=8,'tensor'=4] {'tensor'}, use_global_device_ids=true, to_apply=%region_3.0 | all-reduce | flops 2308 | bytes 18464 | tf_op jit(solution)/shard_map/psum | solution.py:38
  33.9 9.9 all-gather.1
  43.8 38.4 %all-gather.23.cloned.1.call-done = bf16[2,577,1024]{2,1,0:T(8,128)(2,1)} async-done(((bf16[2,577,256]{2,1,0:T(8,128)(2,1)}), bf16[2,577,1024]{2,1,0:T(8,128)(2,1)}) %all-gather.23.cloned.1.call-update) | async-done | bytes 2363408 | tf_op jit(solution)/shard_map/all_gather | solution.py:57
  82.2 3.6 reshape.303
  85.7 22.7 %all-gather.39.cloned.1.call-done = bf16[1,1024,3,256]{3,1,2,0:T(8,128)(2,1)} async-done(((bf16[1,128,3,256]{3,1,2,0:T(8,128)(2,1)}), bf16[1,1024,3,256]{3,1,2,0:T(8,128)(2,1)}) %all-gather.39.cloned.1.call-update) | async-done | bytes 1572880 | tf_op jit(solution)/shard_map/all_gather | solution.py:82
  108.4 4.1 fusion.36
  128.5 3.9 multiply_reduce_fusion.1
  142.3 86.5 %reduce-scatter.13.cloned.1.call-done = f32[2,577,256]{2,1,0:T(8,128)} async-done(((f32[2,577,1024]{2,1,0:T(8,128)}), f32[2,577,256]{2,1,0:T(8,128)}) %reduce-scatter.13.cloned.1.call-update) | async-done | bytes 1181712 | tf_op jit(solution)/shard_map/reduce_scatter | solution.py:61
  230.6 17.9 %all-reduce.7 = (f32[2,577]{1,0:T(2,128)S(1)}, f32[2,577]{1,0:T(2,128)S(1)}) all-reduce(f32[2,577]{1,0:T(2,128)S(1)} %get-tuple-element.93, f32[2,577]{1,0:T(2,128)S(1)} %get-tuple-element.92), channel_id=1, replica_groups=mesh['dp'=8,'tensor'=4] {'tensor'}, use_global_device_ids=true, to_apply=%region_10.0 | all-reduce | flops 2308 | bytes 18464 | tf_op jit(solution)/shard_map/psum | solution.py:38
  253.2 46.1 %all-gather.25.cloned.1.call-done = bf16[2,577,1024]{2,1,0:T(8,128)(2,1)} async-done(((bf16[2,577,256]{2,1,0:T(8,128)(2,1)}), bf16[2,577,1024]{2,1,0:T(8,128)(2,1)}) %all-gather.25.cloned.1.call-update) | async-done | bytes 2363408 | tf_op jit(solution)/shard_map/all_gather | solution.py:57
  299.4 3.6 reshape.282
  302.9 24.7 %all-gather.41.cloned.1.call-done = bf16[1,1024,1024]{2,1,0:T(8,128)(2,1)} async-done(((bf16[1,128,1024]{2,1,0:T(8,128)(2,1)}), bf16[1,1024,1024]{2,1,0:T(8,128)(2,1)}) %all-gather.41.cloned.1.call-update) | async-done | bytes 2097168 | tf_op jit(solution)/shard_map/all_gather | solution.py:84
  327.7 7.1 multiply_convert_fusion.3
  334.8 23.0 %all-gather.43.cloned.1.call-done = bf16[1,1024,1024]{2,1,0:T(8,128)(2,1)} async-done(((bf16[1,128,1024]{2,1,0:T(8,128)(2,1)}), bf16[1,1024,1024]{2,1,0:T(8,128)(2,1)}) %all-gather.43.cloned.1.call-update) | async-done | bytes 2097168 | tf_op jit(solution)/shard_map/all_gather | solution.py:85
  357.8 7.1 fusion.16
  364.9 4.9 reshape.283
  369.9 86.5 %reduce-scatter.15.cloned.1.call-done = f32[2,577,256]{2,1,0:T(8,128)} async-done(((f32[2,577,1024]{2,1,0:T(8,128)}), f32[2,577,256]{2,1,0:T(8,128)}) %reduce-scatter.15.cloned.1.call-update) | async-done | bytes 1181712 | tf_op jit(solution)/shard_map/reduce_scatter | solution.py:61
  458.1 17.9 %all-reduce.6 = (f32[2,577]{1,0:T(2,128)S(1)}, f32[2,577]{1,0:T(2,128)S(1)}) all-reduce(f32[2,577]{1,0:T(2,128)S(1)} %get-tuple-element.91, f32[2,577]{1,0:T(2,128)S(1)} %get-tuple-element.90), channel_id=1, replica_groups=mesh['dp'=8,'tensor'=4] {'tensor'}, use_global_device_ids=true, to_apply=%region_15.0 | all-reduce | flops 2308 | bytes 18464 | tf_op jit(solution)/shard_map/psum | solution.py:38
  478.2 11.1 all-gather.5
  489.3 37.6 %all-gather.27.cloned.1.call-done = bf16[2,577,1024]{2,1,0:T(8,128)(2,1)} async-done(((bf16[2,577,256]{2,1,0:T(8,128)(2,1)}), bf16[2,577,1024]{2,1,0:T(8,128)(2,1)}) %all-gather.27.cloned.1.call-update) | async-done | bytes 2363408 | tf_op jit(solution)/shard_map/all_gather | solution.py:57
  530.4 22.7 %all-gather.45.cloned.1.call-done = bf16[1,1024,3,256]{3,1,2,0:T(8,128)(2,1)} async-done(((bf16[1,128,3,256]{3,1,2,0:T(8,128)(2,1)}), bf16[1,1024,3,256]{3,1,2,0:T(8,128)(2,1)}) %all-gather.45.cloned.1.call-update) | async-done | bytes 1572880 | tf_op jit(solution)/shard_map/all_gather | solution.py:82
  553.2 4.1 fusion.33
  591.3 83.4 %reduce-scatter.17.cloned.1.call-done = f32[2,577,256]{2,1,0:T(8,128)} async-done(((f32[2,577,1024]{2,1,0:T(8,128)}), f32[2,577,256]{2,1,0:T(8,128)}) %reduce-scatter.17.cloned.1.call-update) | async-done | bytes 1181712 | tf_op jit(solution)/shard_map/reduce_scatter | solution.py:61
  677.1 18.6 %all-reduce.5 = (f32[2,577]{1,0:T(2,128)S(1)}, f32[2,577]{1,0:T(2,128)S(1)}) all-reduce(f32[2,577]{1,0:T(2,128)S(1)} %get-tuple-element.89, f32[2,577]{1,0:T(2,128)S(1)} %get-tuple-element.88), channel_id=1, replica_groups=mesh['dp'=8,'tensor'=4] {'tensor'}, use_global_device_ids=true, to_apply=%region_22.0 | all-reduce | flops 2308 | bytes 18464 | tf_op jit(solution)/shard_map/psum | solution.py:38
  700.1 28.4 %all-gather.31.cloned.1.call-done = bf16[2,577,1024]{2,1,0:T(8,128)(2,1)} async-done(((bf16[2,577,256]{2,1,0:T(8,128)(2,1)}), bf16[2,577,1024]{2,1,0:T(8,128)(2,1)}) %all-gather.31.cloned.1.call-update) | async-done | bytes 2363408 | tf_op jit(solution)/shard_map/all_gather | solution.py:65
  732.0 47.8 %all-gather.29.cloned.1.call-done = bf16[2,577,1024]{2,1,0:T(8,128)(2,1)} async-done(((bf16[2,577,256]{2,1,0:T(8,128)(2,1)}), bf16[2,577,1024]{2,1,0:T(8,128)(2,1)}) %all-gather.29.cloned.1.call-update) | async-done | bytes 2363408 | tf_op jit(solution)/shard_map/all_gather | solution.py:57
  779.8 3.6 reshape.285
  783.4 24.9 %all-gather.47.cloned.1.call-done = bf16[1,1024,1024]{2,1,0:T(8,128)(2,1)} async-done(((bf16[1,128,1024]{2,1,0:T(8,128)(2,1)}), bf16[1,1024,1024]{2,1,0:T(8,128)(2,1)}) %all-gather.47.cloned.1.call-update) | async-done | bytes 2097168 | tf_op jit(solution)/shard_map/all_gather | solution.py:84
  808.3 7.2 multiply_convert_fusion.2
  815.5 22.9 %all-gather.49.cloned.1.call-done = bf16[1,1024,1024]{2,1,0:T(8,128)(2,1)} async-done(((bf16[1,128,1024]{2,1,0:T(8,128)(2,1)}), bf16[1,1024,1024]{2,1,0:T(8,128)(2,1)}) %all-gather.49.cloned.1.call-update) | async-done | bytes 2097168 | tf_op jit(solution)/shard_map/all_gather | solution.py:85
  838.4 7.1 fusion.135
  847.0 4.0 convolution_convert_fusion.1
  854.6 7.2 fusion.11
  861.8 5.0 reshape.286
  866.8 36.1 %reduce-scatter.21.cloned.1.call-done = bf16[2,577,256]{2,1,0:T(8,128)(2,1)} async-done(((bf16[2,577,1024]{2,1,0:T(8,128)(2,1)}), bf16[2,577,256]{2,1,0:T(8,128)(2,1)}) %reduce-scatter.21.cloned.1.call-update) | async-done | bytes 590864 | tf_op jit(solution)/shard_map/reduce_scatter | solution.py:69
  905.2 18.0 %all-reduce.4 = (f32[2,577]{1,0:T(2,128)S(1)}, f32[2,577]{1,0:T(2,128)S(1)}) all-reduce(f32[2,577]{1,0:T(2,128)S(1)} %get-tuple-element.83, f32[2,577]{1,0:T(2,128)S(1)} %get-tuple-element.96), channel_id=1, replica_groups=mesh['dp'=8,'tensor'=4] {'tensor'}, use_global_device_ids=true, to_apply=%region_28.0 | all-reduce | flops 2308 | bytes 18464 | tf_op jit(solution)/shard_map/psum | solution.py:49
  923.2 68.0 %reduce-scatter.19.cloned.1.call-done = f32[2,577,256]{2,1,0:T(8,128)} async-done(((f32[2,577,1024]{2,1,0:T(8,128)}), f32[2,577,256]{2,1,0:T(8,128)}) %reduce-scatter.19.cloned.1.call-update) | async-done | bytes 1181712 | tf_op jit(solution)/shard_map/reduce_scatter | solution.py:61
  996.7 51.5 %all-gather.33.cloned.1.call-done = bf16[2,577,1024]{2,1,0:T(8,128)(2,1)} async-done(((bf16[2,577,256]{2,1,0:T(8,128)(2,1)}), bf16[2,577,1024]{2,1,0:T(8,128)(2,1)}) %all-gather.33.cloned.1.call-update) | async-done | bytes 2363408 | tf_op jit(solution)/shard_map/all_gather | solution.py:65
  1061.9 8.6 multiply_convert_fusion.1
  1100.6 4.9 bitcast_convert_fusion.1
  1105.5 3.6 convert_element_type.243
  1109.2 46.6 %reduce-scatter.23.cloned.1.call-done = bf16[2,577,256]{2,1,0:T(8,128)(2,1)} async-done(((bf16[2,577,1024]{2,1,0:T(8,128)(2,1)}), bf16[2,577,256]{2,1,0:T(8,128)(2,1)}) %reduce-scatter.23.cloned.1.call-update) | async-done | bytes 590864 | tf_op jit(solution)/shard_map/reduce_scatter | solution.py:69
  1157.6 17.3 %all-reduce.3 = (f32[2,577]{1,0:T(2,128)S(1)}, f32[2,577]{1,0:T(2,128)S(1)}) all-reduce(f32[2,577]{1,0:T(2,128)S(1)} %get-tuple-element.85, f32[2,577]{1,0:T(2,128)S(1)} %get-tuple-element.95), channel_id=1, replica_groups=mesh['dp'=8,'tensor'=4] {'tensor'}, use_global_device_ids=true, to_apply=%region_34.0 | all-reduce | flops 2308 | bytes 18464 | tf_op jit(solution)/shard_map/psum | solution.py:49
  1179.3 49.1 %all-gather.35.cloned.1.call-done = bf16[2,577,1024]{2,1,0:T(8,128)(2,1)} async-done(((bf16[2,577,256]{2,1,0:T(8,128)(2,1)}), bf16[2,577,1024]{2,1,0:T(8,128)(2,1)}) %all-gather.35.cloned.1.call-update) | async-done | bytes 2363408 | tf_op jit(solution)/shard_map/all_gather | solution.py:65
  1232.0 7.1 fusion.136
  1240.5 3.9 convolution_convert_fusion
  1244.4 3.6 convert_element_type.248
  1248.1 46.6 %reduce-scatter.25.cloned.1.call-done = bf16[2,577,256]{2,1,0:T(8,128)(2,1)} async-done(((bf16[2,577,1024]{2,1,0:T(8,128)(2,1)}), bf16[2,577,256]{2,1,0:T(8,128)(2,1)}) %reduce-scatter.25.cloned.1.call-update) | async-done | bytes 590864 | tf_op jit(solution)/shard_map/reduce_scatter | solution.py:69
  1297.1 17.3 %all-reduce.2 = (f32[2,577]{1,0:T(2,128)S(1)}, f32[2,577]{1,0:T(2,128)S(1)}) all-reduce(f32[2,577]{1,0:T(2,128)S(1)} %get-tuple-element.81, f32[2,577]{1,0:T(2,128)S(1)} %get-tuple-element.97), channel_id=1, replica_groups=mesh['dp'=8,'tensor'=4] {'tensor'}, use_global_device_ids=true, to_apply=%region_39.0 | all-reduce | flops 2308 | bytes 18464 | tf_op jit(solution)/shard_map/psum | solution.py:49
  1319.1 5.5 convert_bitcast_fusion.2
  1330.4 5.5 convert_bitcast_fusion
  1349.4 3.6 fusion.39
  1352.9 14.9 all-gather.37.cloned.1.call-done
  1380.3 6.8 multiply_convert_fusion
  1389.7 7.4 fusion.125
  1397.3 4.0 fusion.126
  1414.8 4.9 bitcast_convert_fusion
  1419.6 3.6 convert_element_type.256
  1432.5 42.5 %reduce-scatter.35.cloned.1.call-done = bf16[2,128,1024]{2,1,0:T(8,128)(2,1)} async-done(((bf16[2,1024,1024]{2,1,0:T(8,128)(2,1)}), bf16[2,128,1024]{2,1,0:T(8,128)(2,1)}) %reduce-scatter.35.cloned.1.call-update) | async-done | bytes 524304 | tf_op jit(solution)/shard_map/reduce_scatter | solution.py:344
  1479.8 34.9 %reduce-scatter.31.cloned.1.call-done = bf16[2,128,256]{2,1,0:T(8,128)(2,1)} async-done(((bf16[2,1024,256]{2,1,0:T(8,128)(2,1)}), bf16[2,128,256]{2,1,0:T(8,128)(2,1)}) %reduce-scatter.31.cloned.1.call-update) | async-done | bytes 131088 | tf_op jit(solution)/shard_map/reduce_scatter | solution.py:344
  1517.4 46.7 %reduce-scatter.29.cloned.1.call-done = bf16[2,128,3,256]{3,1,2,0:T(8,128)(2,1)} async-done(((bf16[2,1024,3,256]{3,1,2,0:T(8,128)(2,1)}), bf16[2,128,3,256]{3,1,2,0:T(8,128)(2,1)}) %reduce-scatter.29.cloned.1.call-update) | async-done | bytes 393232 | tf_op jit(solution)/shard_map/reduce_scatter | solution.py:344
  1568.1 46.5 %reduce-scatter.27.cloned.1.call-done = bf16[2,577,256]{2,1,0:T(8,128)(2,1)} async-done(((bf16[2,577,1024]{2,1,0:T(8,128)(2,1)}), bf16[2,577,256]{2,1,0:T(8,128)(2,1)}) %reduce-scatter.27.cloned.1.call-update) | async-done | bytes 590864 | tf_op jit(solution)/shard_map/reduce_scatter | solution.py:69
  1616.5 17.3 %all-reduce.1 = (f32[2,577]{1,0:T(2,128)S(1)}, f32[2,577]{1,0:T(2,128)S(1)}) all-reduce(f32[2,577]{1,0:T(2,128)S(1)} %get-tuple-element.87, f32[2,577]{1,0:T(2,128)S(1)} %get-tuple-element.94), channel_id=1, replica_groups=mesh['dp'=8,'tensor'=4] {'tensor'}, use_global_device_ids=true, to_apply=%region_45.0 | all-reduce | flops 2308 | bytes 18464 | tf_op jit(solution)/shard_map/psum | solution.py:49
  1637.3 22.4 %all-reduce = (f32[2,8,256]{2,1,0:T(8,128)S(1)}, f32[2,1024]{1,0:T(2,128)S(1)}) all-reduce(f32[2,8,256]{2,1,0:T(8,128)S(1)} %pad_maximum_fusion.9, f32[2,1024]{1,0:T(2,128)S(1)} %pad_maximum_fusion.11), channel_id=1, replica_groups=mesh['dp'=8,'tensor'=4] {'dp'}, use_global_device_ids=true, to_apply=%region_66.0 | all-reduce | flops 6144 | bytes 49152 | tf_op jit(solution)/shard_map/psum | solution.py:346
  (365 shorter events, 239.9 us)
Async XLA Ops:
  7.2 25.6 %copy-start.30 = (f32[2,128,3,256]{3,1,2,0:T(8,128)S(1)}, f32[2,128,3,256]{3,1,2,0:T(8,128)}, u32[]{:S(2)}) copy-start(f32[2,128,3,256]{3,1,2,0:T(8,128)} %param.18) | copy-start | bytes 2359300
  7.2 75.0 %all-gather.23.cloned.1.call-start = ((), (), s32[]{:S(2)}) async-start(), calls=%async_computation.12 | async-start | bytes 2990080 | tf_op jit(solution)/shard_map/all_gather | solution.py:57
  8.3 24.4 %copy-start.65 = (f32[1,1,256]{2,1,0:T(1,128)}, f32[1,1,256]{2,1,0:T(1,128)S(1)}, u32[]{:S(2)}) copy-start(f32[1,1,256]{2,1,0:T(1,128)S(1)} %get-tuple-element.194) | copy-start | bytes 3076
  9.8 24.1 %copy-start.43 = (f32[2,128,256]{2,1,0:T(8,128)S(1)}, f32[2,128,256]{2,1,0:T(8,128)}, u32[]{:S(2)}) copy-start(f32[2,128,256]{2,1,0:T(8,128)} %param.19) | copy-start | bytes 786436
  32.7 75.7 %all-gather.39.cloned.1.call-start = ((), (), s32[]{:S(2)}) async-start(), calls=%async_computation.32 | async-start | bytes 1769472 | tf_op jit(solution)/shard_map/all_gather | solution.py:82
  33.6 195.1 %reduce-scatter.13.cloned.1.call-start = ((), (), s32[]{:S(2)}) async-start(), calls=%async_computation.13 | async-start | bytes 5980160 | tf_op jit(solution)/shard_map/reduce_scatter | solution.py:61
  33.8 94.7 %copy-start.56 = (f32[4,64]{1,0:T(4,128)}, f32[4,64]{1,0:T(4,128)S(1)}, u32[]{:S(2)}) copy-start(f32[4,64]{1,0:T(4,128)S(1)} %add.365) | copy-start | bytes 3076
  33.9 100.7 %copy-start.58 = (f32[4,64]{1,0:T(4,128)}, f32[4,64]{1,0:T(4,128)S(1)}, u32[]{:S(2)}) copy-start(f32[4,64]{1,0:T(4,128)S(1)} %add.362) | copy-start | bytes 3076
  43.8 95.4 %copy-start.37 = (bf16[1,1024,256]{2,1,0:T(8,128)(2,1)}, bf16[1,1024,256]{2,1,0:T(8,128)(2,1)S(1)}, u32[]{:S(2)}) copy-start(bf16[1,1024,256]{2,1,0:T(8,128)(2,1)S(1)} %all-gather.1) | copy-start | bytes 1572868
  117.6 10.9 copy-start.18
  128.5 6.0 copy-start.7
  142.2 86.5 %copy-start.5 = (bf16[2,577,256]{2,0,1:T(2,128)(2,1)S(1)}, bf16[2,577,256]{2,0,1:T(2,128)(2,1)}, u32[]{:S(2)}) copy-start(bf16[2,577,256]{2,0,1:T(2,128)(2,1)} %param.15) | copy-start | bytes 1772548
  142.3 157.1 %all-gather.25.cloned.1.call-start = ((), (), s32[]{:S(2)}) async-start(), calls=%async_computation.14 | async-start | bytes 2990080 | tf_op jit(solution)/shard_map/all_gather | solution.py:57
  228.8 21.1 %copy-start.27 = (f32[2,128,1024]{2,1,0:T(8,128)S(1)}, f32[2,128,1024]{2,1,0:T(8,128)}, u32[]{:S(2)}) copy-start(f32[2,128,1024]{2,1,0:T(8,128)} %param.20) | copy-start | bytes 3145732
  249.8 77.9 %all-gather.41.cloned.1.call-start = ((), (), s32[]{:S(2)}) async-start(), calls=%async_computation.33 | async-start | bytes 2359296 | tf_op jit(solution)/shard_map/all_gather | solution.py:84
  250.8 107.0 %all-gather.43.cloned.1.call-start = ((), (), s32[]{:S(2)}) async-start(), calls=%async_computation.34 | async-start | bytes 2359296 | tf_op jit(solution)/shard_map/all_gather | solution.py:85
  253.0 203.4 %reduce-scatter.15.cloned.1.call-start = ((), (), s32[]{:S(2)}) async-start(), calls=%async_computation.15 | async-start | bytes 5980160 | tf_op jit(solution)/shard_map/reduce_scatter | solution.py:61
  369.9 157.0 %all-gather.27.cloned.1.call-start = ((), (), s32[]{:S(2)}) async-start(), calls=%async_computation.16 | async-start | bytes 2990080 | tf_op jit(solution)/shard_map/all_gather | solution.py:57
  477.3 75.9 %all-gather.45.cloned.1.call-start = ((), (), s32[]{:S(2)}) async-start(), calls=%async_computation.35 | async-start | bytes 1769472 | tf_op jit(solution)/shard_map/all_gather | solution.py:82
  478.0 196.7 %reduce-scatter.17.cloned.1.call-start = ((), (), s32[]{:S(2)}) async-start(), calls=%async_computation.17 | async-start | bytes 5980160 | tf_op jit(solution)/shard_map/reduce_scatter | solution.py:61
  562.4 12.3 copy-start.20
  588.2 140.3 %all-gather.31.cloned.1.call-start = ((), (), s32[]{:S(2)}) async-start(), calls=%async_computation.20 | async-start | bytes 2990080 | tf_op jit(solution)/shard_map/all_gather | solution.py:65
  588.9 402.3 %copy-start.68 = (f32[2]{0:T(128)}, f32[2]{0:T(128)S(1)}, u32[]{:S(2)}) copy-start(f32[2]{0:T(128)S(1)} %add_convert_fusion.15) | copy-start | bytes 28
  591.2 188.6 %all-gather.29.cloned.1.call-start = ((), (), s32[]{:S(2)}) async-start(), calls=%async_computation.18 | async-start | bytes 2990080 | tf_op jit(solution)/shard_map/all_gather | solution.py:57
  698.3 110.0 %all-gather.47.cloned.1.call-start = ((), (), s32[]{:S(2)}) async-start(), calls=%async_computation.36 | async-start | bytes 2359296 | tf_op jit(solution)/shard_map/all_gather | solution.py:84
  699.0 139.4 %all-gather.49.cloned.1.call-start = ((), (), s32[]{:S(2)}) async-start(), calls=%async_computation.37 | async-start | bytes 2359296 | tf_op jit(solution)/shard_map/all_gather | solution.py:85
  699.6 203.3 %reduce-scatter.21.cloned.1.call-start = ((), (), s32[]{:S(2)}) async-start(), calls=%async_computation.21 | async-start | bytes 2990080 | tf_op jit(solution)/shard_map/reduce_scatter | solution.py:69
  838.4 8.6 copy-start.75
  854.5 136.7 %reduce-scatter.19.cloned.1.call-start = ((), (), s32[]{:S(2)}) async-start(), calls=%async_computation.19 | async-start | bytes 5980160 | tf_op jit(solution)/shard_map/reduce_scatter | solution.py:61
  866.8 181.4 %all-gather.33.cloned.1.call-start = ((), (), s32[]{:S(2)}) async-start(), calls=%async_computation.22 | async-start | bytes 2990080 | tf_op jit(solution)/shard_map/all_gather | solution.py:65
  996.6 159.1 %reduce-scatter.23.cloned.1.call-start = ((), (), s32[]{:S(2)}) async-start(), calls=%async_computation.23 | async-start | bytes 2990080 | tf_op jit(solution)/shard_map/reduce_scatter | solution.py:69
  1061.9 8.6 copy-start.21
  1061.9 13.4 slice-start
  1061.9 13.4 slice-start.1
  1109.2 119.3 %all-gather.35.cloned.1.call-start = ((), (), s32[]{:S(2)}) async-start(), calls=%async_computation.24 | async-start | bytes 2990080 | tf_op jit(solution)/shard_map/all_gather | solution.py:65
  1179.3 115.4 %reduce-scatter.25.cloned.1.call-start = ((), (), s32[]{:S(2)}) async-start(), calls=%async_computation.25 | async-start | bytes 2990080 | tf_op jit(solution)/shard_map/reduce_scatter | solution.py:69
  1232.0 8.6 copy-start.74
  1248.0 66.3 %copy-start.16 = (f32[2,577,256]{2,1,0:T(8,128)S(1)}, f32[2,577,256]{2,1,0:T(8,128)}, u32[]{:S(2)}) copy-start(f32[2,577,256]{2,1,0:T(8,128)} %copy-done.15) | copy-start | bytes 3545092
  1248.1 119.7 %all-gather.37.cloned.1.call-start = ((), (), s32[]{:S(2)}) async-start(), calls=%async_computation.26 | async-start | bytes 2990080 | tf_op jit(solution)/shard_map/all_gather | solution.py:65
  1318.7 107.7 %reduce-scatter.33.cloned.1.call-start = ((), (), s32[]{:S(2)}) async-start(), calls=%async_computation.30 | async-start | bytes 4718592 | tf_op jit(solution)/shard_map/reduce_scatter | solution.py:344
  1330.3 144.7 %reduce-scatter.35.cloned.1.call-start = ((), (), s32[]{:S(2)}) async-start(), calls=%async_computation.31 | async-start | bytes 4718592 | tf_op jit(solution)/shard_map/reduce_scatter | solution.py:344
  1341.6 173.1 %reduce-scatter.31.cloned.1.call-start = ((), (), s32[]{:S(2)}) async-start(), calls=%async_computation.29 | async-start | bytes 1179648 | tf_op jit(solution)/shard_map/reduce_scatter | solution.py:344
  1352.9 18.4 %copy-start.38 = (bf16[1,1024,256]{2,1,0:T(8,128)(2,1)S(1)}, bf16[1,1024,256]{2,1,0:T(8,128)(2,1)}, u32[]{:S(2)}) copy-start(bf16[1,1024,256]{2,1,0:T(8,128)(2,1)} %copy-done.37) | copy-start | bytes 1572868
  1380.3 6.9 copy-start.10
  1380.3 6.9 copy-start.57
  1389.7 7.5 copy-start.19
  1397.2 166.9 %reduce-scatter.29.cloned.1.call-start = ((), (), s32[]{:S(2)}) async-start(), calls=%async_computation.28 | async-start | bytes 3538944 | tf_op jit(solution)/shard_map/reduce_scatter | solution.py:344
  1413.3 201.3 %reduce-scatter.27.cloned.1.call-start = ((), (), s32[]{:S(2)}) async-start(), calls=%async_computation.27 | async-start | bytes 2990080 | tf_op jit(solution)/shard_map/reduce_scatter | solution.py:69
  1431.1 43.9 %copy-start.24 = (f32[2,2,128,1024]{3,2,1,0:T(8,128)S(1)}, f32[2,2,128,1024]{3,2,1,0:T(8,128)}, u32[]{:S(2)}) copy-start(f32[2,2,128,1024]{3,2,1,0:T(8,128)} %param.27) | copy-start | bytes 6291460
  1478.2 36.5 %copy-start.41 = (f32[2,2,128,256]{3,2,1,0:T(8,128)S(1)}, f32[2,2,128,256]{3,2,1,0:T(8,128)}, u32[]{:S(2)}) copy-start(f32[2,2,128,256]{3,2,1,0:T(8,128)} %param.25) | copy-start | bytes 1572868
  1478.2 37.4 %copy-start.44 = (f32[2,128,256]{2,1,0:T(8,128)S(1)}, f32[2,128,256]{2,1,0:T(8,128)}, u32[]{:S(2)}) copy-start(f32[2,128,256]{2,1,0:T(8,128)} %param.19) | copy-start | bytes 786436
  1479.6 84.5 %copy-start.29 = (f32[2,2,128,3,256]{4,2,3,1,0:T(8,128)S(1)}, f32[2,2,128,3,256]{4,2,3,1,0:T(8,128)}, u32[]{:S(2)}) copy-start(f32[2,2,128,3,256]{4,2,3,1,0:T(8,128)} %param.24) | copy-start | bytes 4718596
  1515.6 49.6 %copy-start.42 = (f32[2,128,256]{2,1,0:T(8,128)}, f32[2,128,256]{2,1,0:T(8,128)S(1)}, u32[]{:S(2)}) copy-start(f32[2,128,256]{2,1,0:T(8,128)S(1)} %get-tuple-element.131) | copy-start | bytes 786436
  1516.5 48.7 %copy-start.31 = (f32[2,128,3,256]{3,1,2,0:T(8,128)S(1)}, f32[2,128,3,256]{3,1,2,0:T(8,128)}, u32[]{:S(2)}) copy-start(f32[2,128,3,256]{3,1,2,0:T(8,128)} %param.18) | copy-start | bytes 2359300
  1566.8 47.8 %copy-start.6 = (bf16[2,577,256]{2,0,1:T(2,128)(2,1)S(1)}, bf16[2,577,256]{2,0,1:T(2,128)(2,1)}, u32[]{:S(2)}) copy-start(bf16[2,577,256]{2,0,1:T(2,128)(2,1)} %param.15) | copy-start | bytes 1772548
  1566.8 47.8 %copy-start.52 = (f32[2,577]{1,0:T(2,128)S(1)}, f32[2,577]{1,0:T(2,128)}, u32[]{:S(2)}) copy-start(f32[2,577]{1,0:T(2,128)} %copy-done.51) | copy-start | bytes 13852
  1566.8 47.8 %copy-start.54 = (f32[2,577]{1,0:T(2,128)S(1)}, f32[2,577]{1,0:T(2,128)}, u32[]{:S(2)}) copy-start(f32[2,577]{1,0:T(2,128)} %copy-done.53) | copy-start | bytes 13852
  1566.8 47.8 %copy-start.66 = (f32[1,1,256]{2,1,0:T(1,128)S(1)}, f32[1,1,256]{2,1,0:T(1,128)}, u32[]{:S(2)}) copy-start(f32[1,1,256]{2,1,0:T(1,128)} %copy-done.65) | copy-start | bytes 3076
  1566.8 67.0 %copy-start.14 = (f32[2,577,256]{2,1,0:T(8,128)S(1)}, f32[2,577,256]{2,1,0:T(8,128)}, u32[]{:S(2)}) copy-start(f32[2,577,256]{2,1,0:T(8,128)} %copy-done.13) | copy-start | bytes 3545092
  1566.8 67.0 %copy-start.69 = (f32[2]{0:T(128)S(1)}, f32[2]{0:T(128)}, u32[]{:S(2)}) copy-start(f32[2]{0:T(128)} %copy-done.68) | copy-start | bytes 28
  1635.6 24.1 %copy-start.55 = (f32[2,8,256]{2,1,0:T(8,128)S(1)}, f32[2,8,256]{2,1,0:T(8,128)}, u32[]{:S(2)}) copy-start(f32[2,8,256]{2,1,0:T(8,128)} %param.22) | copy-start | bytes 49156
  1635.6 24.1 %copy-start.60 = (f32[2,2,8,256]{3,2,1,0:T(8,128)S(1)}, f32[2,2,8,256]{3,2,1,0:T(8,128)}, u32[]{:S(2)}) copy-start(f32[2,2,8,256]{3,2,1,0:T(8,128)} %param.28) | copy-start | bytes 98308
  1635.6 24.8 %copy-start.62 = (f32[2,1024]{1,0:T(2,128)S(1)}, f32[2,1024]{1,0:T(2,128)}, u32[]{:S(2)}) copy-start(f32[2,1024]{1,0:T(2,128)} %param.23) | copy-start | bytes 24580
  1635.7 24.7 %copy-start.63 = (f32[2,2,1024]{2,1,0:T(2,128)S(1)}, f32[2,2,1024]{2,1,0:T(2,128)}, u32[]{:S(2)}) copy-start(f32[2,2,1024]{2,1,0:T(2,128)} %param.29) | copy-start | bytes 49156
  (46 other events, 123.9 us)
Sparse Core Ops, SparseCore 0:
  32.8 49.2 all-gather.22
  84.6 23.7 all-gather.38
  142.4 86.3 reduce-scatter.12
  249.9 49.3 all-gather.24
  301.7 25.9 all-gather.40
  330.0 27.7 all-gather.42
  370.0 86.3 reduce-scatter.14
  477.4 49.4 all-gather.26
  529.4 23.7 all-gather.44
  588.3 86.3 reduce-scatter.16
  676.8 51.6 all-gather.30
  730.5 49.3 all-gather.28
  782.3 25.9 all-gather.46
  810.6 27.7 all-gather.48
  854.6 48.2 reduce-scatter.20
  905.1 86.0 reduce-scatter.18
  996.8 51.4 all-gather.32
  1109.3 46.4 reduce-scatter.22
  1179.4 48.9 all-gather.34
  1248.2 46.4 reduce-scatter.24
  1318.8 48.9 all-gather.36
  1371.2 49.2 reduce-scatter.32
  1423.8 51.1 reduce-scatter.34
  1478.6 35.9 reduce-scatter.30
  1518.0 46.0 reduce-scatter.28
  1566.3 48.2 reduce-scatter.26
where the time goes:
time: 1680 us; the launch traced here: 1670 us
  waiting for transfers between devices  1080 us (64%)
  blocking collectives  188 us (11%)
  matrix products  160 us (10%)
  local copies, waits for them, and re-layouts  148 us (9%)
  other arithmetic  72.7 us (4%)
    reduce_scatter x4, waiting for transfers between devices, sum_branch(): lax.psum_scatter(partial_rows, 'tensor', scatter_dimension=2, tiled=True)  324 us
    reduce_scatter x4, waiting for transfers between devices, sum_inputs(): lax.psum_scatter(partial_rows.astype(jnp.bfloat16), 'tensor', scatter_dim...  176 us
    all_gather x4, waiting for transfers between devices, share_features(): return lax.all_gather(local_rows, 'tensor', axis=2, tiled=True)  170 us
    all_gather x4, waiting for transfers between devices, share_grads(): return lax.all_gather(local_rows, 'tensor', axis=2, tiled=True)  144 us
    reduce_scatter x4, waiting for transfers between devices, on_device(): lax.psum_scatter(as_sent(stacked), 'dp', scatter_dimension=1, tiled=True)  124 us
    psum x4, blocking collectives, layer_statistics(): lax.psum((jnp.sum(hidden_state, -1), jnp.sum(hidden_state * hidden_state,...  75.1 us
    psum x4, blocking collectives, norm_back(): lax.psum((jnp.sum(d_hat, -1), jnp.sum(d_hat * normed, -1)), 'tensor')  69.8 us
    all_gather x2, waiting for transfers between devices, fetch_weights(): lax.all_gather(pieces[2], 'dp', axis=0, tiled=True)  49.6 us
  transfers between devices with their start and end apart: 26, of which 25 were waited for; matrix products, arithmetic and copies ran while one was open for 10% of the time, Pallas kernels for 0%

commit v1 on v0

--- a/solution.py
+++ b/solution.py
@@ -19,6 +19,22 @@
 CONTRACT_FIRST = (((0,), (0,)), ((), ()))
 
 
+def gather_around(x, axis, dim):
+    ways, here, hop = (lax.axis_size(axis), lax.axis_index(axis), x.shape[dim])
+    lengths = [n * ways if d == dim else n for d, n in enumerate(x.shape)]
+    full = lax.dynamic_update_slice_in_dim(jnp.zeros(lengths, x.dtype), x, here * hop, axis=dim)
+    going_up = going_down = x
+    for far in range(1, ways // 2 + 1):
+        going_up = lax.ppermute(going_up, axis, [(d, (d + 1) % ways) for d in range(ways)])
+        full = lax.dynamic_update_slice_in_dim(full, going_up, (here - far) % ways * hop, axis=dim)
+        if 2 * far < ways:
+            going_down = lax.ppermute(going_down, axis, [(d, (d - 1) % ways) for d in range(ways)])
+            full = lax.dynamic_update_slice_in_dim(
+                full, going_down, (here + far) % ways * hop, axis=dim
+            )
+    return full
+
+
 def as_sent(shard):
     return jax.tree.map(lambda a: a.astype(jnp.bfloat16) if a.dtype == jnp.float32 else a, shard)
 
@@ -54,7 +70,7 @@
 
 
 def share_features(local_rows):
-    return lax.all_gather(local_rows, "tensor", axis=2, tiled=True)
+    return gather_around(local_rows, "tensor", 2)
 
 
 def sum_branch(partial_rows):

time: 1680 us -> 1540 us (0.917)
  waiting for transfers between devices: 1080 us -> 878 us
  starting transfers between devices: 2.52 us -> 40.3 us
  local copies, waits for them, and re-layouts: 148 us -> 176 us
    all_gather x4 -> x0, waiting for transfers between devices: 170 us -> none  [share_features(): return lax.all_gather(local_rows, 'tensor', axis=2, tiled=True)]
    ppermute x0 -> x12, waiting for transfers between devices: none -> 97.2 us  [the longest x8 91.9 us: gather_around(): lax.ppermute(going_up, axis, [(d, (d + 1) % ways) for d in range(ways)])]
    all_gather x2, waiting for transfers between devices: 45.5 us -> 0.01 us  [fetch_weights(): lax.all_gather(pieces[0], 'dp', axis=0, tiled=True)]
    ppermute x0 -> x12, starting transfers between devices: none -> 38.5 us  [the longest x8 21.7 us: gather_around(): lax.ppermute(going_up, axis, [(d, (d + 1) % ways) for d in range(ways)])]
    all_gather x2, waiting for transfers between devices: 49.6 us -> 14.9 us  [fetch_weights(): lax.all_gather(pieces[2], 'dp', axis=0, tiled=True)]
    all_gather x2, waiting for transfers between devices: 45.9 us -> 22.9 us  [fetch_weights(): lax.all_gather(pieces[3], 'dp', axis=0, tiled=True)]
    all_gather x4, waiting for transfers between devices: 144 us -> 123 us  [share_grads(): return lax.all_gather(local_rows, 'tensor', axis=2, tiled=True)]
  transfers between devices with their start and end apart: 26 -> 34, of which waited for: 25 -> 26; matrix products, arithmetic and copies ran while one was open for 10% -> 12% of each run, Pallas kernels for 0% -> 0%
where the time goes in v1:
time: 1540 us; the launch traced here: 1530 us
  waiting for transfers between devices  878 us (57%)
  blocking collectives  191 us (12%)
  local copies, waits for them, and re-layouts  176 us (11%)
  matrix products  160 us (10%)
  other arithmetic  68.9 us (4%)
  starting transfers between devices  40.3 us (3%)
  between operations  16.8 us (1%)
    reduce_scatter x4, waiting for transfers between devices, sum_branch(): lax.psum_scatter(partial_rows, 'tensor', scatter_dimension=2, tiled=True)  313 us
    reduce_scatter x4, waiting for transfers between devices, sum_inputs(): lax.psum_scatter(partial_rows.astype(jnp.bfloat16), 'tensor', scatter_dim...  176 us
    reduce_scatter x4, waiting for transfers between devices, on_device(): lax.psum_scatter(as_sent(stacked), 'dp', scatter_dimension=1, tiled=True)  129 us
    all_gather x4, waiting for transfers between devices, share_grads(): return lax.all_gather(local_rows, 'tensor', axis=2, tiled=True)  123 us
    ppermute x8, waiting for transfers between devices, gather_around(): lax.ppermute(going_up, axis, [(d, (d + 1) % ways) for d in range(ways)])  91.9 us
    psum x4, blocking collectives, layer_statistics(): lax.psum((jnp.sum(hidden_state, -1), jnp.sum(hidden_state * hidden_state,...  76 us
    psum x4, blocking collectives, norm_back(): lax.psum((jnp.sum(d_hat, -1), jnp.sum(d_hat * normed, -1)), 'tensor')  70.2 us
  transfers between devices with their start and end apart: 34, of which 26 were waited for; matrix products, arithmetic and copies ran while one was open for 12% of the time, Pallas kernels for 0%

profile of v1, /device:TPU:0, one launch (start us, length us, event | category | flops | bytes accessed | tf_op | source)
XLA Modules:
  0.0 1530.7 jit_solution(7136484053851594975)
XLA Ops:
  9.8 20.5 %all-reduce.8 = (f32[2,577]{1,0:T(2,128)S(1)}, f32[2,577]{1,0:T(2,128)S(1)}) all-reduce(f32[2,577]{1,0:T(2,128)S(1)} %get-tuple-element.123, f32[2,577]{1,0:T(2,128)S(1)} %get-tuple-element.122), channel_id=1, replica_groups=mesh['dp'=8,'tensor'=4] {'tensor'}, use_global_device_ids=true, to_apply=%region_3.0 | all-reduce | flops 2308 | bytes 18464 | tf_op jit(solution)/shard_map/psum | solution.py:54
  34.6 3.8 collective-permute-start.1
  38.7 14.2 collective-permute-done
  54.3 11.4 all-gather.1
  67.7 5.7 collective-permute-done.2
  77.8 4.1 fusion.36
  97.5 3.9 multiply_reduce_fusion.1
  115.3 81.6 %reduce-scatter.13.cloned.1.call-done = f32[2,577,256]{2,1,0:T(8,128)} async-done(((f32[2,577,1024]{2,1,0:T(8,128)}), f32[2,577,256]{2,1,0:T(8,128)}) %reduce-scatter.13.cloned.1.call-update) | async-done | bytes 1181712 | tf_op jit(solution)/shard_map/reduce_scatter | solution.py:77
  198.5 18.5 %all-reduce.7 = (f32[2,577]{1,0:T(2,128)S(1)}, f32[2,577]{1,0:T(2,128)S(1)}) all-reduce(f32[2,577]{1,0:T(2,128)S(1)} %get-tuple-element.113, f32[2,577]{1,0:T(2,128)S(1)} %get-tuple-element.112), channel_id=1, replica_groups=mesh['dp'=8,'tensor'=4] {'tensor'}, use_global_device_ids=true, to_apply=%region_10.11 | all-reduce | flops 2308 | bytes 18464 | tf_op jit(solution)/shard_map/psum | solution.py:54
  220.6 3.8 collective-permute-start.4
  224.4 14.2 collective-permute-done.3
  242.4 5.3 collective-permute-done.4
  248.7 10.5 collective-permute-done.5
  260.2 3.6 reshape.282
  263.8 7.2 multiply_convert_fusion.3
  270.9 7.1 fusion.16
  278.1 4.9 reshape.283
  283.6 84.0 %reduce-scatter.15.cloned.1.call-done = f32[2,577,256]{2,1,0:T(8,128)} async-done(((f32[2,577,1024]{2,1,0:T(8,128)}), f32[2,577,256]{2,1,0:T(8,128)}) %reduce-scatter.15.cloned.1.call-update) | async-done | bytes 1181712 | tf_op jit(solution)/shard_map/reduce_scatter | solution.py:77
  369.4 18.0 %all-reduce.6 = (f32[2,577]{1,0:T(2,128)S(1)}, f32[2,577]{1,0:T(2,128)S(1)}) all-reduce(f32[2,577]{1,0:T(2,128)S(1)} %get-tuple-element.111, f32[2,577]{1,0:T(2,128)S(1)} %get-tuple-element.110), channel_id=1, replica_groups=mesh['dp'=8,'tensor'=4] {'tensor'}, use_global_device_ids=true, to_apply=%region_15.16 | all-reduce | flops 2308 | bytes 18464 | tf_op jit(solution)/shard_map/psum | solution.py:54
  391.6 3.8 collective-permute-start.7
  395.6 14.2 collective-permute-done.6
  412.4 11.5 all-gather.5
  435.0 4.1 fusion.33
  474.4 80.3 %reduce-scatter.17.cloned.1.call-done = f32[2,577,256]{2,1,0:T(8,128)} async-done(((f32[2,577,1024]{2,1,0:T(8,128)}), f32[2,577,256]{2,1,0:T(8,128)}) %reduce-scatter.17.cloned.1.call-update) | async-done | bytes 1181712 | tf_op jit(solution)/shard_map/reduce_scatter | solution.py:77
  557.1 19.1 %all-reduce.5 = (f32[2,577]{1,0:T(2,128)S(1)}, f32[2,577]{1,0:T(2,128)S(1)}) all-reduce(f32[2,577]{1,0:T(2,128)S(1)} %get-tuple-element.109, f32[2,577]{1,0:T(2,128)S(1)} %get-tuple-element.108), channel_id=1, replica_groups=mesh['dp'=8,'tensor'=4] {'tensor'}, use_global_device_ids=true, to_apply=%region_22.23 | all-reduce | flops 2308 | bytes 18464 | tf_op jit(solution)/shard_map/psum | solution.py:54
  582.3 5.4 collective-permute-start.10
  587.6 27.2 %collective-permute-done.9 = bf16[2,577,256]{2,0,1:T(2,128)(2,1)} collective-permute-done((bf16[2,577,256]{2,0,1:T(2,128)(2,1)}, bf16[2,577,256]{2,0,1:T(2,128)(2,1)}, u32[]{:S(2)}, u32[]{:S(2)}) %collective-permute-start.9) | collective-permute-done | bytes 590880 | tf_op jit(solution)/shard_map/ppermute | solution.py:28
  614.8 13.1 collective-permute-start.11
  627.9 8.4 all-gather.19.cloned.1.call-done
  651.9 14.9 all-gather.35.cloned.1.call-done
  666.8 7.2 multiply_convert_fusion.2
  674.0 22.9 %all-gather.37.cloned.1.call-done = bf16[1,1024,1024]{2,1,0:T(8,128)(2,1)} async-done(((bf16[1,128,1024]{2,1,0:T(8,128)(2,1)}), bf16[1,1024,1024]{2,1,0:T(8,128)(2,1)}) %all-gather.37.cloned.1.call-update) | async-done | bytes 2097168 | tf_op jit(solution)/shard_map/all_gather | solution.py:101
  697.0 7.7 fusion.136
  706.1 4.0 convolution_convert_fusion.1
  713.7 7.2 fusion.11
  720.9 5.0 reshape.286
  725.9 36.1 %reduce-scatter.21.cloned.1.call-done = bf16[2,577,256]{2,1,0:T(8,128)(2,1)} async-done(((bf16[2,577,1024]{2,1,0:T(8,128)(2,1)}), bf16[2,577,256]{2,1,0:T(8,128)(2,1)}) %reduce-scatter.21.cloned.1.call-update) | async-done | bytes 590864 | tf_op jit(solution)/shard_map/reduce_scatter | solution.py:85
  764.8 18.4 %all-reduce.4 = (f32[2,577]{1,0:T(2,128)S(1)}, f32[2,577]{1,0:T(2,128)S(1)}) all-reduce(f32[2,577]{1,0:T(2,128)S(1)} %get-tuple-element.103, f32[2,577]{1,0:T(2,128)S(1)} %get-tuple-element.116), channel_id=1, replica_groups=mesh['dp'=8,'tensor'=4] {'tensor'}, use_global_device_ids=true, to_apply=%region_28.29 | all-reduce | flops 2308 | bytes 18464 | tf_op jit(solution)/shard_map/psum | solution.py:65
  783.2 67.2 %reduce-scatter.19.cloned.1.call-done = f32[2,577,256]{2,1,0:T(8,128)} async-done(((f32[2,577,1024]{2,1,0:T(8,128)}), f32[2,577,256]{2,1,0:T(8,128)}) %reduce-scatter.19.cloned.1.call-update) | async-done | bytes 1181712 | tf_op jit(solution)/shard_map/reduce_scatter | solution.py:77
  850.4 4.1 fusion.120
  856.5 51.6 %all-gather.21.cloned.1.call-done = bf16[2,577,1024]{2,1,0:T(8,128)(2,1)} async-done(((bf16[2,577,256]{2,1,0:T(8,128)(2,1)}), bf16[2,577,1024]{2,1,0:T(8,128)(2,1)}) %all-gather.21.cloned.1.call-update) | async-done | bytes 2363408 | tf_op jit(solution)/shard_map/all_gather | solution.py:81
  921.6 8.6 multiply_convert_fusion.1
  935.6 3.8 fusion.128
  961.4 5.0 bitcast_convert_fusion.1
  970.0 46.6 %reduce-scatter.23.cloned.1.call-done = bf16[2,577,256]{2,1,0:T(8,128)(2,1)} async-done(((bf16[2,577,1024]{2,1,0:T(8,128)(2,1)}), bf16[2,577,256]{2,1,0:T(8,128)(2,1)}) %reduce-scatter.23.cloned.1.call-update) | async-done | bytes 590864 | tf_op jit(solution)/shard_map/reduce_scatter | solution.py:85
  1019.0 17.3 %all-reduce.3 = (f32[2,577]{1,0:T(2,128)S(1)}, f32[2,577]{1,0:T(2,128)S(1)}) all-reduce(f32[2,577]{1,0:T(2,128)S(1)} %get-tuple-element.105, f32[2,577]{1,0:T(2,128)S(1)} %get-tuple-element.115), channel_id=1, replica_groups=mesh['dp'=8,'tensor'=4] {'tensor'}, use_global_device_ids=true, to_apply=%region_34.35 | all-reduce | flops 2308 | bytes 18464 | tf_op jit(solution)/shard_map/psum | solution.py:65
  1040.7 49.1 %all-gather.23.cloned.1.call-done = bf16[2,577,1024]{2,1,0:T(8,128)(2,1)} async-done(((bf16[2,577,256]{2,1,0:T(8,128)(2,1)}), bf16[2,577,1024]{2,1,0:T(8,128)(2,1)}) %all-gather.23.cloned.1.call-update) | async-done | bytes 2363408 | tf_op jit(solution)/shard_map/all_gather | solution.py:81
  1093.3 7.7 fusion.137
  1102.4 3.9 convolution_convert_fusion
  1110.0 46.6 %reduce-scatter.25.cloned.1.call-done = bf16[2,577,256]{2,1,0:T(8,128)(2,1)} async-done(((bf16[2,577,1024]{2,1,0:T(8,128)(2,1)}), bf16[2,577,256]{2,1,0:T(8,128)(2,1)}) %reduce-scatter.25.cloned.1.call-update) | async-done | bytes 590864 | tf_op jit(solution)/shard_map/reduce_scatter | solution.py:85
  1159.0 17.3 %all-reduce.2 = (f32[2,577]{1,0:T(2,128)S(1)}, f32[2,577]{1,0:T(2,128)S(1)}) all-reduce(f32[2,577]{1,0:T(2,128)S(1)} %get-tuple-element.101, f32[2,577]{1,0:T(2,128)S(1)} %get-tuple-element.117), channel_id=1, replica_groups=mesh['dp'=8,'tensor'=4] {'tensor'}, use_global_device_ids=true, to_apply=%region_39.40 | all-reduce | flops 2308 | bytes 18464 | tf_op jit(solution)/shard_map/psum | solution.py:65
  1180.3 5.5 convert_bitcast_fusion.2
  1193.1 5.0 convert_bitcast_fusion
  1215.2 13.8 all-gather.25.cloned.1.call-done
  1242.1 6.7 multiply_convert_fusion
  1251.3 7.4 fusion.126
  1258.8 4.0 fusion.127
  1275.1 4.0 bitcast_convert_fusion
  1288.8 47.2 %reduce-scatter.35.cloned.1.call-done = bf16[2,128,1024]{2,1,0:T(8,128)(2,1)} async-done(((bf16[2,1024,1024]{2,1,0:T(8,128)(2,1)}), bf16[2,128,1024]{2,1,0:T(8,128)(2,1)}) %reduce-scatter.35.cloned.1.call-update) | async-done | bytes 524304 | tf_op jit(solution)/shard_map/reduce_scatter | solution.py:360
  1340.7 34.8 %reduce-scatter.31.cloned.1.call-done = bf16[2,128,256]{2,1,0:T(8,128)(2,1)} async-done(((bf16[2,1024,256]{2,1,0:T(8,128)(2,1)}), bf16[2,128,256]{2,1,0:T(8,128)(2,1)}) %reduce-scatter.31.cloned.1.call-update) | async-done | bytes 131088 | tf_op jit(solution)/shard_map/reduce_scatter | solution.py:360
  1378.3 46.7 %reduce-scatter.29.cloned.1.call-done = bf16[2,128,3,256]{3,1,2,0:T(8,128)(2,1)} async-done(((bf16[2,1024,3,256]{3,1,2,0:T(8,128)(2,1)}), bf16[2,128,3,256]{3,1,2,0:T(8,128)(2,1)}) %reduce-scatter.29.cloned.1.call-update) | async-done | bytes 393232 | tf_op jit(solution)/shard_map/reduce_scatter | solution.py:360
  1429.0 46.6 %reduce-scatter.27.cloned.1.call-done = bf16[2,577,256]{2,1,0:T(8,128)(2,1)} async-done(((bf16[2,577,1024]{2,1,0:T(8,128)(2,1)}), bf16[2,577,256]{2,1,0:T(8,128)(2,1)}) %reduce-scatter.27.cloned.1.call-update) | async-done | bytes 590864 | tf_op jit(solution)/shard_map/reduce_scatter | solution.py:85
  1477.5 17.3 %all-reduce.1 = (f32[2,577]{1,0:T(2,128)S(1)}, f32[2,577]{1,0:T(2,128)S(1)}) all-reduce(f32[2,577]{1,0:T(2,128)S(1)} %get-tuple-element.107, f32[2,577]{1,0:T(2,128)S(1)} %get-tuple-element.114), channel_id=1, replica_groups=mesh['dp'=8,'tensor'=4] {'tensor'}, use_global_device_ids=true, to_apply=%region_45.46 | all-reduce | flops 2308 | bytes 18464 | tf_op jit(solution)/shard_map/psum | solution.py:65
  1498.4 22.4 %all-reduce = (f32[2,8,256]{2,1,0:T(8,128)S(1)}, f32[2,1024]{1,0:T(2,128)S(1)}) all-reduce(f32[2,8,256]{2,1,0:T(8,128)S(1)} %pad_maximum_fusion.9, f32[2,1024]{1,0:T(2,128)S(1)} %pad_maximum_fusion.11), channel_id=1, replica_groups=mesh['dp'=8,'tensor'=4] {'dp'}, use_global_device_ids=true, to_apply=%region_66.67 | all-reduce | flops 6144 | bytes 49152 | tf_op jit(solution)/shard_map/psum | solution.py:362
  (427 shorter events, 291.2 us)
Async XLA Ops:
  7.2 23.0 %copy-start.59 = (f32[2,8,256]{2,1,0:T(8,128)S(1)}, f32[2,8,256]{2,1,0:T(8,128)}, u32[]{:S(2)}) copy-start(f32[2,8,256]{2,1,0:T(8,128)} %param.22) | copy-start | bytes 49156
  7.2 70.6 %all-gather.27.cloned.1.call-start = ((), (), s32[]{:S(2)}) async-start(), calls=%async_computation.28 | async-start | bytes 1769472 | tf_op jit(solution)/shard_map/all_gather | solution.py:98
  9.3 187.5 %reduce-scatter.13.cloned.1.call-start = ((), (), s32[]{:S(2)}) async-start(), calls=%async_computation.12 | async-start | bytes 5980160 | tf_op jit(solution)/shard_map/reduce_scatter | solution.py:77
  34.6 18.2 %collective-permute-start = (bf16[2,577,256]{2,0,1:T(2,128)(2,1)}, bf16[2,577,256]{2,0,1:T(2,128)(2,1)S(1)}, u32[]{:S(2)}, u32[]{:S(2)}) collective-permute-start(bf16[2,577,256]{2,0,1:T(2,128)(2,1)} %copy.192), channel_id=1, source_target_pairs={{0,1},{1,2},{2,3},{3,0},{4,5},{5,6},{6,7},{7,4},{8,9},{9,10},{10,1... | collective-permute-start | bytes 1772552 | tf_op jit(solution)/shard_map/ppermute | solution.py:28
  34.6 32.1 %collective-permute-start.1 = (bf16[2,577,256]{2,0,1:T(2,128)(2,1)}, bf16[2,577,256]{2,0,1:T(2,128)(2,1)S(1)}, u32[]{:S(2)}, u32[]{:S(2)}) collective-permute-start(bf16[2,577,256]{2,0,1:T(2,128)(2,1)} %copy.192), channel_id=1, source_target_pairs={{0,3},{1,0},{2,1},{3,2},{4,7},{5,4},{6,5},{7,6},{8,11},{9,8},{10,9... | collective-permute-start | bytes 1772552 | tf_op jit(solution)/shard_map/ppermute | solution.py:31
  38.5 59.0 %copy-start.61 = (f32[4,64]{1,0:T(4,128)}, f32[4,64]{1,0:T(4,128)S(1)}, u32[]{:S(2)}) copy-start(f32[4,64]{1,0:T(4,128)S(1)} %add.424) | copy-start | bytes 3076
  38.6 65.0 %copy-start.63 = (f32[4,64]{1,0:T(4,128)}, f32[4,64]{1,0:T(4,128)S(1)}, u32[]{:S(2)}) copy-start(f32[4,64]{1,0:T(4,128)S(1)} %add.421) | copy-start | bytes 3076
  52.8 20.5 %collective-permute-start.2 = (bf16[2,577,256]{2,0,1:T(2,128)(2,1)S(1)}, bf16[2,577,256]{2,0,1:T(2,128)(2,1)S(1)}, u32[]{:S(2)}, u32[]{:S(2)}) collective-permute-start(bf16[2,577,256]{2,0,1:T(2,128)(2,1)S(1)} %collective-permute-done), channel_id=1, source_target_pairs={{0,1},{1,2},{2,3},{3,0},{4,5},{5,6},{6,7},{7,4},{8,9},{9,10},{10,1... | collective-permute-start | bytes 1772552 | tf_op jit(solution)/shard_map/ppermute | solution.py:28
  65.7 42.5 %copy-start.41 = (bf16[1,1024,256]{2,1,0:T(8,128)(2,1)}, bf16[1,1024,256]{2,1,0:T(8,128)(2,1)S(1)}, u32[]{:S(2)}) copy-start(bf16[1,1024,256]{2,1,0:T(8,128)(2,1)S(1)} %all-gather.1) | copy-start | bytes 1572868
  86.7 10.8 copy-start.19
  112.1 151.6 %all-gather.29.cloned.1.call-start = ((), (), s32[]{:S(2)}) async-start(), calls=%async_computation.29 | async-start | bytes 2359296 | tf_op jit(solution)/shard_map/all_gather | solution.py:100
  114.2 156.7 %all-gather.31.cloned.1.call-start = ((), (), s32[]{:S(2)}) async-start(), calls=%async_computation.30 | async-start | bytes 2359296 | tf_op jit(solution)/shard_map/all_gather | solution.py:101
  115.2 252.4 %reduce-scatter.15.cloned.1.call-start = ((), (), s32[]{:S(2)}) async-start(), calls=%async_computation.13 | async-start | bytes 5980160 | tf_op jit(solution)/shard_map/reduce_scatter | solution.py:77
  218.8 22.7 %copy-start.66 = (f32[2,1024]{1,0:T(2,128)S(1)}, f32[2,1024]{1,0:T(2,128)}, u32[]{:S(2)}) copy-start(f32[2,1024]{1,0:T(2,128)} %param.23) | copy-start | bytes 24580
  220.5 18.1 %collective-permute-start.3 = (bf16[2,577,256]{2,0,1:T(2,128)(2,1)S(1)}, bf16[2,577,256]{2,0,1:T(2,128)(2,1)S(1)}, u32[]{:S(2)}, u32[]{:S(2)}) collective-permute-start(bf16[2,577,256]{2,0,1:T(2,128)(2,1)S(1)} %copy.205), channel_id=1, source_target_pairs={{0,1},{1,2},{2,3},{3,0},{4,5},{5,6},{6,7},{7,4},{8,9},{9,10},{10,1... | collective-permute-start | bytes 1772552 | tf_op jit(solution)/shard_map/ppermute | solution.py:28
  220.6 27.1 %collective-permute-start.4 = (bf16[2,577,256]{2,0,1:T(2,128)(2,1)S(1)}, bf16[2,577,256]{2,0,1:T(2,128)(2,1)S(1)}, u32[]{:S(2)}, u32[]{:S(2)}) collective-permute-start(bf16[2,577,256]{2,0,1:T(2,128)(2,1)S(1)} %copy.205), channel_id=1, source_target_pairs={{0,3},{1,0},{2,1},{3,2},{4,7},{5,4},{6,5},{7,6},{8,11},{9,8},{10,9... | collective-permute-start | bytes 1772552 | tf_op jit(solution)/shard_map/ppermute | solution.py:31
  238.6 20.6 %collective-permute-start.5 = (bf16[2,577,256]{2,0,1:T(2,128)(2,1)S(1)}, bf16[2,577,256]{2,0,1:T(2,128)(2,1)S(1)}, u32[]{:S(2)}, u32[]{:S(2)}) collective-permute-start(bf16[2,577,256]{2,0,1:T(2,128)(2,1)S(1)} %collective-permute-done.3), channel_id=1, source_target_pairs={{0,1},{1,2},{2,3},{3,0},{4,5},{5,6},{6,7},{7,4},{8,9},{9,10},{10,1... | collective-permute-start | bytes 1772552 | tf_op jit(solution)/shard_map/ppermute | solution.py:28
  283.0 152.0 %all-gather.33.cloned.1.call-start = ((), (), s32[]{:S(2)}) async-start(), calls=%async_computation.31 | async-start | bytes 1769472 | tf_op jit(solution)/shard_map/all_gather | solution.py:98
  283.6 271.1 %reduce-scatter.17.cloned.1.call-start = ((), (), s32[]{:S(2)}) async-start(), calls=%async_computation.14 | async-start | bytes 5980160 | tf_op jit(solution)/shard_map/reduce_scatter | solution.py:77
  391.6 18.2 %collective-permute-start.6 = (bf16[2,577,256]{2,0,1:T(2,128)(2,1)}, bf16[2,577,256]{2,0,1:T(2,128)(2,1)S(1)}, u32[]{:S(2)}, u32[]{:S(2)}) collective-permute-start(bf16[2,577,256]{2,0,1:T(2,128)(2,1)} %copy.210), channel_id=1, source_target_pairs={{0,1},{1,2},{2,3},{3,0},{4,5},{5,6},{6,7},{7,4},{8,9},{9,10},{10,1... | collective-permute-start | bytes 1772552 | tf_op jit(solution)/shard_map/ppermute | solution.py:28
  391.6 33.3 %collective-permute-start.7 = (bf16[2,577,256]{2,0,1:T(2,128)(2,1)}, bf16[2,577,256]{2,0,1:T(2,128)(2,1)}, u32[]{:S(2)}, u32[]{:S(2)}) collective-permute-start(bf16[2,577,256]{2,0,1:T(2,128)(2,1)} %copy.210), channel_id=1, source_target_pairs={{0,3},{1,0},{2,1},{3,2},{4,7},{5,4},{6,5},{7,6},{8,11},{9,8},{10,9... | collective-permute-start | bytes 1772552 | tf_op jit(solution)/shard_map/ppermute | solution.py:31
  409.9 20.6 %collective-permute-start.8 = (bf16[2,577,256]{2,0,1:T(2,128)(2,1)S(1)}, bf16[2,577,256]{2,0,1:T(2,128)(2,1)S(1)}, u32[]{:S(2)}, u32[]{:S(2)}) collective-permute-start(bf16[2,577,256]{2,0,1:T(2,128)(2,1)S(1)} %collective-permute-done.6), channel_id=1, source_target_pairs={{0,1},{1,2},{2,3},{3,0},{4,5},{5,6},{6,7},{7,4},{8,9},{9,10},{10,1... | collective-permute-start | bytes 1772552 | tf_op jit(solution)/shard_map/ppermute | solution.py:28
  444.2 12.3 copy-start.21
  470.0 166.3 %all-gather.19.cloned.1.call-start = ((), (), s32[]{:S(2)}) async-start(), calls=%async_computation.16 | async-start | bytes 2990080 | tf_op jit(solution)/shard_map/all_gather | solution.py:81
  470.7 379.7 %copy-start.75 = (f32[2]{0:T(128)}, f32[2]{0:T(128)S(1)}, u32[]{:S(2)}) copy-start(f32[2]{0:T(128)S(1)} %add_convert_fusion.15) | copy-start | bytes 28
  473.0 193.8 %all-gather.35.cloned.1.call-start = ((), (), s32[]{:S(2)}) async-start(), calls=%async_computation.32 | async-start | bytes 2359296 | tf_op jit(solution)/shard_map/all_gather | solution.py:100
  473.7 223.2 %all-gather.37.cloned.1.call-start = ((), (), s32[]{:S(2)}) async-start(), calls=%async_computation.33 | async-start | bytes 2359296 | tf_op jit(solution)/shard_map/all_gather | solution.py:101
  474.3 287.7 %reduce-scatter.21.cloned.1.call-start = ((), (), s32[]{:S(2)}) async-start(), calls=%async_computation.17 | async-start | bytes 2990080 | tf_op jit(solution)/shard_map/reduce_scatter | solution.py:85
  580.6 34.2 %collective-permute-start.9 = (bf16[2,577,256]{2,0,1:T(2,128)(2,1)}, bf16[2,577,256]{2,0,1:T(2,128)(2,1)}, u32[]{:S(2)}, u32[]{:S(2)}) collective-permute-start(bf16[2,577,256]{2,0,1:T(2,128)(2,1)} %copy.223), channel_id=1, source_target_pairs={{0,1},{1,2},{2,3},{3,0},{4,5},{5,6},{6,7},{7,4},{8,9},{9,10},{10,1... | collective-permute-start | bytes 1772552 | tf_op jit(solution)/shard_map/ppermute | solution.py:28
  582.3 59.6 %collective-permute-start.10 = (bf16[2,577,256]{2,0,1:T(2,128)(2,1)}, bf16[2,577,256]{2,0,1:T(2,128)(2,1)}, u32[]{:S(2)}, u32[]{:S(2)}) collective-permute-start(bf16[2,577,256]{2,0,1:T(2,128)(2,1)} %copy.223), channel_id=1, source_target_pairs={{0,3},{1,0},{2,1},{3,2},{4,7},{5,4},{6,5},{7,6},{8,11},{9,8},{10,9... | collective-permute-start | bytes 1772552 | tf_op jit(solution)/shard_map/ppermute | solution.py:31
  614.8 31.5 %collective-permute-start.11 = (bf16[2,577,256]{2,0,1:T(2,128)(2,1)}, bf16[2,577,256]{2,0,1:T(2,128)(2,1)}, u32[]{:S(2)}, u32[]{:S(2)}) collective-permute-start(bf16[2,577,256]{2,0,1:T(2,128)(2,1)} %collective-permute-done.9), channel_id=1, source_target_pairs={{0,1},{1,2},{2,3},{3,0},{4,5},{5,6},{6,7},{7,4},{8,9},{9,10},{10,1... | collective-permute-start | bytes 1772552 | tf_op jit(solution)/shard_map/ppermute | solution.py:28
  697.0 9.2 copy-start.90
  713.6 136.8 %reduce-scatter.19.cloned.1.call-start = ((), (), s32[]{:S(2)}) async-start(), calls=%async_computation.15 | async-start | bytes 5980160 | tf_op jit(solution)/shard_map/reduce_scatter | solution.py:77
  725.9 182.1 %all-gather.21.cloned.1.call-start = ((), (), s32[]{:S(2)}) async-start(), calls=%async_computation.18 | async-start | bytes 2990080 | tf_op jit(solution)/shard_map/all_gather | solution.py:81
  856.4 160.2 %reduce-scatter.23.cloned.1.call-start = ((), (), s32[]{:S(2)}) async-start(), calls=%async_computation.19 | async-start | bytes 2990080 | tf_op jit(solution)/shard_map/reduce_scatter | solution.py:85
  921.6 8.6 copy-start.22
  921.6 14.0 slice-start
  921.6 14.0 slice-start.1
  970.0 119.8 %all-gather.23.cloned.1.call-start = ((), (), s32[]{:S(2)}) async-start(), calls=%async_computation.20 | async-start | bytes 2990080 | tf_op jit(solution)/shard_map/all_gather | solution.py:81
  1040.6 116.0 %reduce-scatter.25.cloned.1.call-start = ((), (), s32[]{:S(2)}) async-start(), calls=%async_computation.21 | async-start | bytes 2990080 | tf_op jit(solution)/shard_map/reduce_scatter | solution.py:85
  1093.3 9.2 copy-start.89
  1110.0 119.0 %all-gather.25.cloned.1.call-start = ((), (), s32[]{:S(2)}) async-start(), calls=%async_computation.22 | async-start | bytes 2990080 | tf_op jit(solution)/shard_map/all_gather | solution.py:81
  1179.8 104.4 %reduce-scatter.33.cloned.1.call-start = ((), (), s32[]{:S(2)}) async-start(), calls=%async_computation.26 | async-start | bytes 4718592 | tf_op jit(solution)/shard_map/reduce_scatter | solution.py:360
  1191.5 144.5 %reduce-scatter.35.cloned.1.call-start = ((), (), s32[]{:S(2)}) async-start(), calls=%async_computation.27 | async-start | bytes 4718592 | tf_op jit(solution)/shard_map/reduce_scatter | solution.py:360
  1203.8 171.8 %reduce-scatter.31.cloned.1.call-start = ((), (), s32[]{:S(2)}) async-start(), calls=%async_computation.25 | async-start | bytes 1179648 | tf_op jit(solution)/shard_map/reduce_scatter | solution.py:360
  1215.1 17.4 %copy-start.42 = (bf16[1,1024,256]{2,1,0:T(8,128)(2,1)S(1)}, bf16[1,1024,256]{2,1,0:T(8,128)(2,1)}, u32[]{:S(2)}) copy-start(bf16[1,1024,256]{2,1,0:T(8,128)(2,1)} %copy-done.41) | copy-start | bytes 1572868
  1258.8 166.3 %reduce-scatter.29.cloned.1.call-start = ((), (), s32[]{:S(2)}) async-start(), calls=%async_computation.24 | async-start | bytes 3538944 | tf_op jit(solution)/shard_map/reduce_scatter | solution.py:360
  1274.8 200.9 %reduce-scatter.27.cloned.1.call-start = ((), (), s32[]{:S(2)}) async-start(), calls=%async_computation.23 | async-start | bytes 2990080 | tf_op jit(solution)/shard_map/reduce_scatter | solution.py:85
  1287.3 48.6 %copy-start.25 = (f32[2,2,128,1024]{3,2,1,0:T(8,128)S(1)}, f32[2,2,128,1024]{3,2,1,0:T(8,128)}, u32[]{:S(2)}) copy-start(f32[2,2,128,1024]{3,2,1,0:T(8,128)} %param.27) | copy-start | bytes 6291460
  1339.1 36.5 %copy-start.45 = (f32[2,2,128,256]{3,2,1,0:T(8,128)S(1)}, f32[2,2,128,256]{3,2,1,0:T(8,128)}, u32[]{:S(2)}) copy-start(f32[2,2,128,256]{3,2,1,0:T(8,128)} %param.25) | copy-start | bytes 1572868
  1339.1 37.4 %copy-start.48 = (f32[2,128,256]{2,1,0:T(8,128)S(1)}, f32[2,128,256]{2,1,0:T(8,128)}, u32[]{:S(2)}) copy-start(f32[2,128,256]{2,1,0:T(8,128)} %param.19) | copy-start | bytes 786436
  1340.6 84.5 %copy-start.32 = (f32[2,2,128,3,256]{4,2,3,1,0:T(8,128)S(1)}, f32[2,2,128,3,256]{4,2,3,1,0:T(8,128)}, u32[]{:S(2)}) copy-start(f32[2,2,128,3,256]{4,2,3,1,0:T(8,128)} %param.24) | copy-start | bytes 4718596
  1376.5 49.7 %copy-start.46 = (f32[2,128,256]{2,1,0:T(8,128)}, f32[2,128,256]{2,1,0:T(8,128)S(1)}, u32[]{:S(2)}) copy-start(f32[2,128,256]{2,1,0:T(8,128)S(1)} %get-tuple-element.151) | copy-start | bytes 786436
  1377.5 48.7 %copy-start.33 = (f32[2,128,3,256]{3,1,2,0:T(8,128)S(1)}, f32[2,128,3,256]{3,1,2,0:T(8,128)}, u32[]{:S(2)}) copy-start(f32[2,128,3,256]{3,1,2,0:T(8,128)} %param.18) | copy-start | bytes 2359300
  1427.7 47.9 %copy-start.7 = (bf16[2,577,256]{2,0,1:T(2,128)(2,1)S(1)}, bf16[2,577,256]{2,0,1:T(2,128)(2,1)}, u32[]{:S(2)}) copy-start(bf16[2,577,256]{2,0,1:T(2,128)(2,1)} %param.15) | copy-start | bytes 1772548
  1427.7 47.9 %copy-start.56 = (f32[2,577]{1,0:T(2,128)S(1)}, f32[2,577]{1,0:T(2,128)}, u32[]{:S(2)}) copy-start(f32[2,577]{1,0:T(2,128)} %copy-done.55) | copy-start | bytes 13852
  1427.7 47.9 %copy-start.58 = (f32[2,577]{1,0:T(2,128)S(1)}, f32[2,577]{1,0:T(2,128)}, u32[]{:S(2)}) copy-start(f32[2,577]{1,0:T(2,128)} %copy-done.57) | copy-start | bytes 13852
  1427.7 47.9 %copy-start.71 = (f32[1,1,256]{2,1,0:T(1,128)S(1)}, f32[1,1,256]{2,1,0:T(1,128)}, u32[]{:S(2)}) copy-start(f32[1,1,256]{2,1,0:T(1,128)} %copy-done.70) | copy-start | bytes 3076
  1427.7 67.1 %copy-start.15 = (f32[2,577,256]{2,1,0:T(8,128)S(1)}, f32[2,577,256]{2,1,0:T(8,128)}, u32[]{:S(2)}) copy-start(f32[2,577,256]{2,1,0:T(8,128)} %copy-done.14) | copy-start | bytes 3545092
  1427.7 67.1 %copy-start.76 = (f32[2]{0:T(128)S(1)}, f32[2]{0:T(128)}, u32[]{:S(2)}) copy-start(f32[2]{0:T(128)} %copy-done.75) | copy-start | bytes 28
  1496.7 24.1 %copy-start.60 = (f32[2,8,256]{2,1,0:T(8,128)S(1)}, f32[2,8,256]{2,1,0:T(8,128)}, u32[]{:S(2)}) copy-start(f32[2,8,256]{2,1,0:T(8,128)} %param.22) | copy-start | bytes 49156
  1496.7 24.1 %copy-start.65 = (f32[2,2,8,256]{3,2,1,0:T(8,128)S(1)}, f32[2,2,8,256]{3,2,1,0:T(8,128)}, u32[]{:S(2)}) copy-start(f32[2,2,8,256]{3,2,1,0:T(8,128)} %param.28) | copy-start | bytes 98308
  1496.7 24.8 %copy-start.67 = (f32[2,1024]{1,0:T(2,128)S(1)}, f32[2,1024]{1,0:T(2,128)}, u32[]{:S(2)}) copy-start(f32[2,1024]{1,0:T(2,128)} %param.23) | copy-start | bytes 24580
  1496.7 24.7 %copy-start.68 = (f32[2,2,1024]{2,1,0:T(2,128)S(1)}, f32[2,2,1024]{2,1,0:T(2,128)}, u32[]{:S(2)}) copy-start(f32[2,2,1024]{2,1,0:T(2,128)} %param.29) | copy-start | bytes 49156
  (69 other events, 205.8 us)
Sparse Core Ops, SparseCore 0:
  10.5 28.2 all-gather.26
  112.2 84.5 reduce-scatter.12
  199.3 28.2 all-gather.28
  229.9 27.7 all-gather.30
  283.1 84.4 reduce-scatter.14
  370.0 26.0 all-gather.32
  470.1 84.5 reduce-scatter.16
  556.8 79.4 all-gather.18
  638.7 28.0 all-gather.34
  669.1 27.7 all-gather.36
  713.8 48.2 reduce-scatter.20
  764.2 86.1 reduce-scatter.18
  856.5 51.4 all-gather.20
  970.1 46.4 reduce-scatter.22
  1040.8 48.9 all-gather.22
  1110.1 46.4 reduce-scatter.24
  1179.9 48.9 all-gather.24
  1232.1 49.2 reduce-scatter.32
  1284.8 51.0 reduce-scatter.34
  1339.6 35.9 reduce-scatter.30
  1379.0 46.0 reduce-scatter.28
  1427.4 48.2 reduce-scatter.26
